TPU v7x, 32 devices: a whole 2x2x4 slice. The times are simulated.
32 devices in a mesh: pb: 4 (over y, core), ma: 8 (over z, x).
Axes of the slice: x: 2, y: 2, z: 4, core: 2. Of those that a mesh axis runs over, the one named last changes fastest.
Arguments:
- queries: bfloat16 [1, 1024, 2048], P(None, ('pb', 'ma')), may hold values from -6 to 6
- map_descriptors: bfloat16 [8192, 2048], P('ma', 'pb'), may hold values from -0.125 to 0.125
- slopes: int32 [8], replicated, may hold values from 0 to 15, as said below
Outputs:
- best: float32 [1, 1024, 8192], P(None, 'pb', 'ma')
Inputs may be any that keep to these rules, and one draw needn't show every extreme that they name: `slopes`: 8 distinct velocities; the largest is exactly 15.
All inputs are finite; a program needn't handle non-finite values.
Results may differ from a plain program's by a relative error of at most 0.0003.
Values may be sent and summed in bfloat16 or wider, within the bound.
A program may use at most 64 MiB of HBM per device.

v0:
```python
import math
import jax
import jax.numpy as jnp
from jax import lax
from jax.sharding import PartitionSpec as P

SEQ = 20
RAD = 10
SPAN = 285


def padded(value, sides, width):
    for axis, dim in sides:
        peers, length = (lax.axis_size(axis), value.shape[dim])
        up = [(i, (i + 1) % peers) for i in range(peers - 1)]
        down = [(j, i) for i, j in up]
        last = lax.slice_in_dim(value, length - width, length, axis=dim)
        leading = lax.slice_in_dim(value, 0, width, axis=dim)
        before = lax.ppermute(last, axis, up)
        after = lax.ppermute(leading, axis, down)
        value = jnp.concatenate([before, value, after], axis=dim)
    return value


def passed_along(value, axis, by):
    peers = lax.axis_size(axis)
    pairs = [(i, i + by) for i in range(peers) if 0 <= i + by < peers]
    return lax.ppermute(value, axis, pairs)


def score_tile(queries, map_descriptors):
    query_full = lax.all_gather(queries, "ma", axis=1, tiled=True)
    return jnp.einsum(
        "sqd,md->sqm",
        query_full,
        lax.all_gather(map_descriptors, "pb", axis=1, tiled=True),
        preferred_element_type=jnp.float32,
    )


def contrast(extended, columns):
    shape_out = (extended.shape[0], extended.shape[1], columns)
    running = jnp.zeros(shape_out, jnp.float32)
    squares = jnp.zeros(shape_out, jnp.float32)
    for offset in range(2 * RAD + 1):
        window = extended[:, :, offset : offset + columns]
        running = running + window
        squares = squares + window * window
    average = running / (2 * RAD + 1)
    spread = squares / (2 * RAD + 1) - average * average
    centre = extended[:, :, RAD : RAD + columns]
    return (centre - average) / jnp.sqrt(spread + 1.0)


def sequence_best(normal_ext, slopes, q_count, m_count):
    sessions = normal_ext.shape[0]
    best_val = None
    for slope_index in range(slopes.shape[0]):
        velocity = slopes[slope_index]
        summed = jnp.zeros((sessions, q_count, m_count), jnp.float32)
        for lag_step in range(SEQ):
            row_at = jnp.asarray(SEQ - 1 - lag_step, jnp.int32)
            col_at = SPAN - lag_step * velocity
            zero_at = jnp.asarray(0, jnp.int32)
            summed = summed + lax.dynamic_slice(
                normal_ext, (zero_at, row_at, col_at), (sessions, q_count, m_count)
            )
        best_val = summed if best_val is None else jnp.maximum(best_val, summed)
    return best_val / math.sqrt(SEQ)


def local(queries, map_descriptors, slopes):
    m_count = map_descriptors.shape[0]
    lead_rows = SEQ - 1
    scores = score_tile(queries, map_descriptors)
    q_count = scores.shape[1]
    widened = padded(scores, (("ma", 2),), RAD)
    normal = contrast(widened, m_count)
    before = passed_along(normal[:, :, m_count - SPAN :], "ma", 1)
    normal_ext = jnp.concatenate([before, normal], axis=2)
    above = passed_along(normal_ext[:, q_count - lead_rows :], "pb", 1)
    normal_ext = jnp.concatenate([above, normal_ext], axis=1)
    return sequence_best(normal_ext, slopes, q_count, m_count)


def solution(mesh):
    return jax.shard_map(
        local,
        mesh=mesh,
        in_specs=(P(None, ("pb", "ma"), None), P("ma", "pb"), P()),
        out_specs=P(None, "pb", "ma"),
        check_vma=False,
    )
```

profile of v0, /device:TPU:1, one launch (start us, length us, event | category | flops | bytes accessed | tf_op | source)
XLA Modules:
  0.0 369.5 jit_solution(10224925232081690869)
XLA Ops:
  6.5 0.0 all-gather.3.cloned.1.call-start
  6.5 0.7 all-gather.3.cloned.1.call-update
  7.3 0.0 all-gather.5.cloned.1.call-start
  7.3 0.7 all-gather.5.cloned.1.call-update
  8.0 42.1 %all-gather.3.cloned.1.call-done = bf16[1,256,2048]{2,1,0:T(8,128)(2,1)} async-done(((bf16[1,32,2048]{2,1,0:T(8,128)(2,1)}), bf16[1,256,2048]{2,1,0:T(8,128)(2,1)}) %all-gather.3.cloned.1.call-update) | async-done | bytes 1048592 | tf_op jit(solution)/shard_map/all_gather | solution.py:32
  50.1 36.9 %all-gather.5.cloned.1.call-done = bf16[1024,2048]{1,0:T(8,128)(2,1)} async-done(((bf16[1024,512]{1,0:T(8,128)(2,1)}), bf16[1024,2048]{1,0:T(8,128)(2,1)}) %all-gather.5.cloned.1.call-update) | async-done | bytes 4194320 | tf_op jit(solution)/shard_map/all_gather | solution.py:36
  87.0 3.8 %fusion.345 = f32[256,1024]{1,0:T(8,128)S(1)} fusion(bf16[1024,2048]{1,0:T(8,128)(2,1)} %all-gather.5.cloned.1.call-done, bf16[1,256,2048]{2,1,0:T(8,128)(2,1)} %all-gather.3.cloned.1.call-done), kind=kOutput, calls=%fused_computation.539 | convolution fusion | flops 1073741824 | bytes 6291456 | tf_op jit(solution)/shard_map/sqd,md->sqm/dot_general | solution.py:33
  90.8 0.1 fusion.348
  90.9 3.1 collective-permute-start
  94.0 0.0 copy-start
  94.0 1.3 collective-permute-start.1
  95.3 1.2 collective-permute-done
  96.6 3.9 %collective-permute-done.1 = f32[1,256,10]{2,1,0:T(8,128)S(1)} collective-permute-done((f32[1,256,10]{2,1,0:T(8,128)S(1)}, f32[1,256,10]{2,1,0:T(8,128)S(1)}, u32[]{:S(2)}, u32[]{:S(2)}) %collective-permute-start.1) | collective-permute-done | bytes 10272 | tf_op jit(solution)/shard_map/ppermute | solution.py:20
  100.4 7.6 %fusion.344 = f32[1,256,1024]{2,1,0:T(8,128)S(1)} fusion(f32[256,1024]{1,0:T(8,128)S(1)} %fusion.345, f32[1,256,1024]{2,1,0:T(8,128)S(1)} %bitcast.342, f32[1,256,10]{2,1,0:T(8,128)S(1)} %collective-permute-done.1, f32[1,256,10]{2,1,0:T(8,128)S(1)} %collective-permute-done), kind=kLoop, calls=%fused_computation.538 | loop fusion | flops 23068672 | bytes 3166208 | tf_op jit(solution)/shard_map/div | solution.py:52
  108.0 0.2 slice.186
  108.2 4.0 %collective-permute-start.2 = (f32[1,256,285]{2,1,0:T(8,128)S(1)}, f32[1,256,285]{2,1,0:T(8,128)S(1)}, u32[]{:S(2)}, u32[]{:S(2)}) collective-permute-start(f32[1,256,285]{2,1,0:T(8,128)S(1)} %slice.186), channel_id=1, source_target_pairs={{0,1},{1,2},{2,3},{3,4},{4,5},{5,6},{6,7},{8,9},{9,10},{10,11},{11... | collective-permute-start | bytes 875528 | tf_op jit(solution)/shard_map/ppermute | solution.py:28
  112.2 0.0 copy-done
  112.2 0.7 fusion.349
  215.6 0.0 collective-permute-done.2
  215.6 0.1 fusion.347
  215.8 3.8 %collective-permute-start.3 = (f32[1,19,1309]{2,1,0:T(8,128)S(1)}, f32[1,19,1309]{2,1,0:T(8,128)S(1)}, u32[]{:S(2)}, u32[]{:S(2)}) collective-permute-start(f32[1,19,1309]{2,1,0:T(8,128)S(1)} %fusion.347), channel_id=1, source_target_pairs={{0,8},{8,16},{16,24},{1,9},{9,17},{17,25},{2,10},{10,18},{18,26},{... | collective-permute-start | bytes 298460 | tf_op jit(solution)/shard_map/ppermute | solution.py:28
  219.5 0.4 pad_maximum_fusion
  219.9 1.6 collective-permute-done.3
  221.5 141.2 %fusion.21 = f32[1,256,1024]{2,1,0:T(8,128)} fusion(s32[]{:T(128)S(6)} %select_n.607, f32[1,19,1309]{2,1,0:T(8,128)S(1)} %collective-permute-done.3, f32[1,256,1024]{2,1,0:T(8,128)S(1)} %fusion.344, s32[]{:T(128)S(6)} %select_n.532, s32[]{:T(128)S(6)} %select_n.533, s32[]{:T(128)S(6)} %select_n.534, s32[]{:T(128)S(6)} %select_n.535, s32[]{:T(128)S(6)} %select_n.536, ...), kind=kLoop, calls=%fused_computation.212 | loop fusion | flops 81788928 | bytes 3537660 | tf_op jit(solution)/shard_map/div | solution.py:69
Async XLA Ops:
  6.5 43.6 %all-gather.3.cloned.1.call-start = ((), (), s32[]{:S(2)}) async-start(), calls=%async_computation | async-start | bytes 1179648 | tf_op jit(solution)/shard_map/all_gather | solution.py:32
  7.3 79.7 %all-gather.5.cloned.1.call-start = ((), (), s32[]{:S(2)}) async-start(), calls=%async_computation.1 | async-start | bytes 5242880 | tf_op jit(solution)/shard_map/all_gather | solution.py:36
  90.9 5.7 %collective-permute-start = (f32[1,256,10]{2,1,0:T(8,128)S(1)}, f32[1,256,10]{2,1,0:T(8,128)S(1)}, u32[]{:S(2)}, u32[]{:S(2)}) collective-permute-start(f32[1,256,10]{2,1,0:T(8,128)S(1)} %get-tuple-element.5), channel_id=1, source_target_pairs={{0,1},{1,2},{2,3},{3,4},{4,5},{5,6},{6,7},{8,9},{9,10},{10,11},{11... | collective-permute-start | bytes 30728 | tf_op jit(solution)/shard_map/ppermute | solution.py:19
  94.0 18.2 %copy-start = (s32[8]{0:T(128)S(1)}, s32[8]{0:T(128)}, u32[]{:S(2)}) copy-start(s32[8]{0:T(128)} %param.5) | copy-start | bytes 100
  94.0 6.4 %collective-permute-start.1 = (f32[1,256,10]{2,1,0:T(8,128)S(1)}, f32[1,256,10]{2,1,0:T(8,128)S(1)}, u32[]{:S(2)}, u32[]{:S(2)}) collective-permute-start(f32[1,256,10]{2,1,0:T(8,128)S(1)} %get-tuple-element.6), channel_id=1, source_target_pairs={{1,0},{2,1},{3,2},{4,3},{5,4},{6,5},{7,6},{9,8},{10,9},{11,10},{12... | collective-permute-start | bytes 30728 | tf_op jit(solution)/shard_map/ppermute | solution.py:20
  108.2 107.5 %collective-permute-start.2 = (f32[1,256,285]{2,1,0:T(8,128)S(1)}, f32[1,256,285]{2,1,0:T(8,128)S(1)}, u32[]{:S(2)}, u32[]{:S(2)}) collective-permute-start(f32[1,256,285]{2,1,0:T(8,128)S(1)} %slice.186), channel_id=1, source_target_pairs={{0,1},{1,2},{2,3},{3,4},{4,5},{5,6},{6,7},{8,9},{9,10},{10,11},{11... | collective-permute-start | bytes 875528 | tf_op jit(solution)/shard_map/ppermute | solution.py:28
  215.8 5.7 %collective-permute-start.3 = (f32[1,19,1309]{2,1,0:T(8,128)S(1)}, f32[1,19,1309]{2,1,0:T(8,128)S(1)}, u32[]{:S(2)}, u32[]{:S(2)}) collective-permute-start(f32[1,19,1309]{2,1,0:T(8,128)S(1)} %fusion.347), channel_id=1, source_target_pairs={{0,8},{8,16},{16,24},{1,9},{9,17},{17,25},{2,10},{10,18},{18,26},{... | collective-permute-start | bytes 298460 | tf_op jit(solution)/shard_map/ppermute | solution.py:28
Sparse Core Ops, SparseCore 0:
  9.5 40.6 all-gather.2
  51.7 35.2 all-gather.4
where the time goes:
time: 371 us; the launch traced here: 370 us
  other arithmetic  149 us (40%)
  between operations  116 us (31%)
  waiting for transfers between devices  87.1 us (23%)
  starting transfers between devices  12.2 us (3%)
  matrix products  3.79 us (1%)
    div x1, other arithmetic, sequence_best(): return best_val / math.sqrt(SEQ)  141 us
    all_gather x1, waiting for transfers between devices, score_tile(): query_full = lax.all_gather(queries, 'ma', axis=1, tiled=True)  42.1 us
    all_gather x1, waiting for transfers between devices, score_tile(): lax.all_gather(map_descriptors, 'pb', axis=1, tiled=True)  36.9 us
    ppermute x2, starting transfers between devices, passed_along(): return lax.ppermute(value, axis, pairs)  7.78 us
    div x1, other arithmetic, contrast(): return (centre - average) / jnp.sqrt(spread + 1.0)  7.57 us
  transfers between devices with their start and end apart: 6, of which 5 were waited for; matrix products, arithmetic and copies ran while one was open for 0% of the time, Pallas kernels for 0%

commit v1 on v0

--- a/solution.py
+++ b/solution.py
@@ -7,6 +7,22 @@
 SEQ = 20
 RAD = 10
 SPAN = 285
+
+
+def ring_gather(x, axis, dim):
+    ways, here, hop = (lax.axis_size(axis), lax.axis_index(axis), x.shape[dim])
+    shape = [n * ways if d == dim else n for d, n in enumerate(x.shape)]
+    full = lax.dynamic_update_slice_in_dim(jnp.zeros(shape, x.dtype), x, here * hop, axis=dim)
+    going_up = going_down = x
+    for far in range(1, ways // 2 + 1):
+        going_up = lax.ppermute(going_up, axis, [(d, (d + 1) % ways) for d in range(ways)])
+        full = lax.dynamic_update_slice_in_dim(full, going_up, (here - far) % ways * hop, axis=dim)
+        if 2 * far < ways:
+            going_down = lax.ppermute(going_down, axis, [(d, (d - 1) % ways) for d in range(ways)])
+            full = lax.dynamic_update_slice_in_dim(
+                full, going_down, (here + far) % ways * hop, axis=dim
+            )
+    return full
 
 
 def padded(value, sides, width):
@@ -29,7 +45,7 @@
 
 
 def score_tile(queries, map_descriptors):
-    query_full = lax.all_gather(queries, "ma", axis=1, tiled=True)
+    query_full = ring_gather(queries, "ma", 1)
     return jnp.einsum(
         "sqd,md->sqm",
         query_full,

time: 371 us -> 329 us (0.89)
  waiting for transfers between devices: 87.1 us -> 31.6 us
  starting transfers between devices: 12.2 us -> 26.1 us
    all_gather x1 -> x0, waiting for transfers between devices: 42.1 us -> none  [score_tile(): query_full = lax.all_gather(queries, 'ma', axis=1, tiled=True)]
    all_gather x1, waiting for transfers between devices: 36.9 us -> 10.4 us  [score_tile(): lax.all_gather(map_descriptors, 'pb', axis=1, tiled=True)]
    ppermute x0 -> x7, starting transfers between devices: none -> 13.9 us  [the longest x3 11.9 us: ring_gather(): lax.ppermute(going_down, axis, [(d, (d - 1) % ways) for d in range(ways)])]
    ppermute x0 -> x7, waiting for transfers between devices: none -> 13.8 us  [the longest x4 13.8 us: ring_gather(): lax.ppermute(going_up, axis, [(d, (d + 1) % ways) for d in range(ways)])]
  transfers between devices with their start and end apart: 6 -> 12, of which waited for: 5 -> 8; matrix products, arithmetic and copies ran while one was open for 0% -> 0% of each run, Pallas kernels for 0% -> 0%
where the time goes in v1:
time: 329 us; the launch traced here: 327 us
  other arithmetic  149 us (45%)
  between operations  116 us (35%)
  waiting for transfers between devices  31.6 us (10%)
  starting transfers between devices  26.1 us (8%)
  matrix products  3.46 us (1%)
    div x1, other arithmetic, sequence_best(): return best_val / math.sqrt(SEQ)  141 us
    ppermute x4, waiting for transfers between devices, ring_gather(): lax.ppermute(going_up, axis, [(d, (d + 1) % ways) for d in range(ways)])  13.8 us
    ppermute x3, starting transfers between devices, ring_gather(): lax.ppermute(going_down, axis, [(d, (d - 1) % ways) for d in range(ways)])  11.9 us
    all_gather x1, waiting for transfers between devices, score_tile(): lax.all_gather(map_descriptors, 'pb', axis=1, tiled=True)  10.4 us
    ppermute x2, starting transfers between devices, passed_along(): return lax.ppermute(value, axis, pairs)  7.78 us
    div x1, other arithmetic, contrast(): return (centre - average) / jnp.sqrt(spread + 1.0)  7.57 us
  transfers between devices with their start and end apart: 12, of which 8 were waited for; matrix products, arithmetic and copies ran while one was open for 0% of the time, Pallas kernels for 0%

profile of v1, /device:TPU:1, one launch (start us, length us, event | category | flops | bytes accessed | tf_op | source)
XLA Modules:
  0.0 327.2 jit_solution(874782434138649852)
XLA Ops:
  6.5 0.0 copy-start
  6.5 0.0 all-gather.2.cloned.1.call-start
  6.5 0.7 all-gather.2.cloned.1.call-update
  7.3 2.1 collective-permute-start
  9.3 3.1 collective-permute-start.1
  12.4 0.1 broadcast.17
  12.6 0.0 copy-done
  12.7 3.1 collective-permute-done
  15.8 0.0 collective-permute-start.2
  15.8 0.0 collective-permute-done.1
  15.8 4.2 %collective-permute-start.3 = (bf16[1,32,2048]{2,1,0:T(8,128)(2,1)S(1)}, bf16[1,32,2048]{2,1,0:T(8,128)(2,1)S(1)}, u32[]{:S(2)}, u32[]{:S(2)}) collective-permute-start(bf16[1,32,2048]{2,1,0:T(8,128)(2,1)S(1)} %collective-permute-done.1), channel_id=1, source_target_pairs={{0,7},{1,0},{2,1},{3,2},{4,3},{5,4},{6,5},{7,6},{8,15},{9,8},{10,9... | collective-permute-start | bytes 393224 | tf_op jit(solution)/shard_map/ppermute | solution.py:21
  20.0 2.4 collective-permute-done.2
  22.4 0.0 collective-permute-start.4
  22.4 0.0 collective-permute-done.3
  22.4 4.6 %collective-permute-start.5 = (bf16[1,32,2048]{2,1,0:T(8,128)(2,1)S(1)}, bf16[1,32,2048]{2,1,0:T(8,128)(2,1)S(1)}, u32[]{:S(2)}, u32[]{:S(2)}) collective-permute-start(bf16[1,32,2048]{2,1,0:T(8,128)(2,1)S(1)} %collective-permute-done.3), channel_id=1, source_target_pairs={{0,7},{1,0},{2,1},{3,2},{4,3},{5,4},{6,5},{7,6},{8,15},{9,8},{10,9... | collective-permute-start | bytes 393224 | tf_op jit(solution)/shard_map/ppermute | solution.py:21
  27.0 1.9 collective-permute-done.4
  28.9 0.0 collective-permute-start.6
  28.9 0.0 collective-permute-done.5
  29.0 6.5 %collective-permute-done.6 = bf16[1,32,2048]{2,1,0:T(8,128)(2,1)S(1)} collective-permute-done((bf16[1,32,2048]{2,1,0:T(8,128)(2,1)S(1)}, bf16[1,32,2048]{2,1,0:T(8,128)(2,1)S(1)}, u32[]{:S(2)}, u32[]{:S(2)}) %collective-permute-start.6) | collective-permute-done | bytes 131104 | tf_op jit(solution)/shard_map/ppermute | solution.py:18
  35.4 10.4 %all-gather.2.cloned.1.call-done = bf16[1024,2048]{1,0:T(8,128)(2,1)} async-done(((bf16[1024,512]{1,0:T(8,128)(2,1)}), bf16[1024,2048]{1,0:T(8,128)(2,1)}) %all-gather.2.cloned.1.call-update) | async-done | bytes 4194320 | tf_op jit(solution)/shard_map/all_gather | solution.py:52
  45.9 3.5 %fusion.348 = f32[256,1024]{1,0:T(8,128)S(1)} fusion(bf16[256,2048]{1,0:T(8,128)(2,1)S(1)} %bitcast_dynamic-update-slice_fusion, bf16[1024,2048]{1,0:T(8,128)(2,1)} %all-gather.2.cloned.1.call-done), kind=kOutput, calls=%fused_computation.606 | convolution fusion | flops 1073741824 | bytes 6291456 | tf_op jit(solution)/shard_map/sqd,md->sqm/dot_general | solution.py:49
  49.3 0.1 fusion.346
  49.4 3.1 collective-permute-start.7
  52.5 0.0 copy-start.1
  52.5 1.3 collective-permute-start.8
  53.8 1.2 collective-permute-done.7
  55.1 3.9 %collective-permute-done.8 = f32[1,256,10]{2,1,0:T(8,128)S(1)} collective-permute-done((f32[1,256,10]{2,1,0:T(8,128)S(1)}, f32[1,256,10]{2,1,0:T(8,128)S(1)}, u32[]{:S(2)}, u32[]{:S(2)}) %collective-permute-start.8) | collective-permute-done | bytes 10272 | tf_op jit(solution)/shard_map/ppermute | solution.py:36
  58.9 7.6 %fusion.344 = f32[1,256,1024]{2,1,0:T(8,128)S(1)} fusion(f32[256,1024]{1,0:T(8,128)S(1)} %fusion.348, f32[1,256,1024]{2,1,0:T(8,128)S(1)} %bitcast.356, f32[1,256,10]{2,1,0:T(8,128)S(1)} %collective-permute-done.8, f32[1,256,10]{2,1,0:T(8,128)S(1)} %collective-permute-done.7), kind=kLoop, calls=%fused_computation.538 | loop fusion | flops 23068672 | bytes 3166208 | tf_op jit(solution)/shard_map/div | solution.py:68
  66.5 0.2 slice.186
  66.7 4.0 %collective-permute-start.9 = (f32[1,256,285]{2,1,0:T(8,128)S(1)}, f32[1,256,285]{2,1,0:T(8,128)S(1)}, u32[]{:S(2)}, u32[]{:S(2)}) collective-permute-start(f32[1,256,285]{2,1,0:T(8,128)S(1)} %slice.186), channel_id=1, source_target_pairs={{0,1},{1,2},{2,3},{3,4},{4,5},{5,6},{6,7},{8,9},{9,10},{10,11},{11... | collective-permute-start | bytes 875528 | tf_op jit(solution)/shard_map/ppermute | solution.py:44
  70.7 0.0 copy-done.1
  70.7 0.7 fusion.347
  173.3 0.0 collective-permute-done.9
  173.3 0.1 fusion.345
  173.4 3.8 %collective-permute-start.10 = (f32[1,19,1309]{2,1,0:T(8,128)S(1)}, f32[1,19,1309]{2,1,0:T(8,128)S(1)}, u32[]{:S(2)}, u32[]{:S(2)}) collective-permute-start(f32[1,19,1309]{2,1,0:T(8,128)S(1)} %fusion.345), channel_id=1, source_target_pairs={{0,8},{8,16},{16,24},{1,9},{9,17},{17,25},{2,10},{10,18},{18,26},{... | collective-permute-start | bytes 298460 | tf_op jit(solution)/shard_map/ppermute | solution.py:44
  177.2 0.4 pad_maximum_fusion
  177.6 1.6 collective-permute-done.10
  179.2 141.2 %fusion.21 = f32[1,256,1024]{2,1,0:T(8,128)} fusion(s32[]{:T(128)S(6)} %select_n.677, f32[1,19,1309]{2,1,0:T(8,128)S(1)} %collective-permute-done.10, f32[1,256,1024]{2,1,0:T(8,128)S(1)} %fusion.344, s32[]{:T(128)S(6)} %select_n.602, s32[]{:T(128)S(6)} %select_n.603, s32[]{:T(128)S(6)} %select_n.604, s32[]{:T(128)S(6)} %select_n.605, s32[]{:T(128)S(6)} %select_n.606, ...), kind=kLoop, calls=%fused_computation.212 | loop fusion | flops 81788928 | bytes 3537660 | tf_op jit(solution)/shard_map/div | solution.py:85
  (8 shorter events, 0.1 us)
Async XLA Ops:
  6.5 6.0 %copy-start = (bf16[1,32,2048]{2,1,0:T(8,128)(2,1)S(1)}, bf16[1,32,2048]{2,1,0:T(8,128)(2,1)}, u32[]{:S(2)}) copy-start(bf16[1,32,2048]{2,1,0:T(8,128)(2,1)} %param.3) | copy-start | bytes 393220
  6.5 39.3 %all-gather.2.cloned.1.call-start = ((), (), s32[]{:S(2)}) async-start(), calls=%async_computation | async-start | bytes 5242880 | tf_op jit(solution)/shard_map/all_gather | solution.py:52
  7.3 8.5 %collective-permute-start = (bf16[1,32,2048]{2,1,0:T(8,128)(2,1)}, bf16[1,32,2048]{2,1,0:T(8,128)(2,1)S(1)}, u32[]{:S(2)}, u32[]{:S(2)}) collective-permute-start(bf16[1,32,2048]{2,1,0:T(8,128)(2,1)} %param.3), channel_id=1, source_target_pairs={{0,1},{1,2},{2,3},{3,4},{4,5},{5,6},{6,7},{7,0},{8,9},{9,10},{10,1... | collective-permute-start | bytes 393224 | tf_op jit(solution)/shard_map/ppermute | solution.py:18
  9.3 6.5 %collective-permute-start.1 = (bf16[1,32,2048]{2,1,0:T(8,128)(2,1)}, bf16[1,32,2048]{2,1,0:T(8,128)(2,1)S(1)}, u32[]{:S(2)}, u32[]{:S(2)}) collective-permute-start(bf16[1,32,2048]{2,1,0:T(8,128)(2,1)} %param.3), channel_id=1, source_target_pairs={{0,7},{1,0},{2,1},{3,2},{4,3},{5,4},{6,5},{7,6},{8,15},{9,8},{10,9... | collective-permute-start | bytes 393224 | tf_op jit(solution)/shard_map/ppermute | solution.py:21
  15.8 6.6 %collective-permute-start.2 = (bf16[1,32,2048]{2,1,0:T(8,128)(2,1)S(1)}, bf16[1,32,2048]{2,1,0:T(8,128)(2,1)S(1)}, u32[]{:S(2)}, u32[]{:S(2)}) collective-permute-start(bf16[1,32,2048]{2,1,0:T(8,128)(2,1)S(1)} %collective-permute-done), channel_id=1, source_target_pairs={{0,1},{1,2},{2,3},{3,4},{4,5},{5,6},{6,7},{7,0},{8,9},{9,10},{10,1... | collective-permute-start | bytes 393224 | tf_op jit(solution)/shard_map/ppermute | solution.py:18
  15.8 6.6 %collective-permute-start.3 = (bf16[1,32,2048]{2,1,0:T(8,128)(2,1)S(1)}, bf16[1,32,2048]{2,1,0:T(8,128)(2,1)S(1)}, u32[]{:S(2)}, u32[]{:S(2)}) collective-permute-start(bf16[1,32,2048]{2,1,0:T(8,128)(2,1)S(1)} %collective-permute-done.1), channel_id=1, source_target_pairs={{0,7},{1,0},{2,1},{3,2},{4,3},{5,4},{6,5},{7,6},{8,15},{9,8},{10,9... | collective-permute-start | bytes 393224 | tf_op jit(solution)/shard_map/ppermute | solution.py:21
  22.4 6.5 %collective-permute-start.4 = (bf16[1,32,2048]{2,1,0:T(8,128)(2,1)S(1)}, bf16[1,32,2048]{2,1,0:T(8,128)(2,1)S(1)}, u32[]{:S(2)}, u32[]{:S(2)}) collective-permute-start(bf16[1,32,2048]{2,1,0:T(8,128)(2,1)S(1)} %collective-permute-done.2), channel_id=1, source_target_pairs={{0,1},{1,2},{2,3},{3,4},{4,5},{5,6},{6,7},{7,0},{8,9},{9,10},{10,1... | collective-permute-start | bytes 393224 | tf_op jit(solution)/shard_map/ppermute | solution.py:18
  22.4 6.5 %collective-permute-start.5 = (bf16[1,32,2048]{2,1,0:T(8,128)(2,1)S(1)}, bf16[1,32,2048]{2,1,0:T(8,128)(2,1)S(1)}, u32[]{:S(2)}, u32[]{:S(2)}) collective-permute-start(bf16[1,32,2048]{2,1,0:T(8,128)(2,1)S(1)} %collective-permute-done.3), channel_id=1, source_target_pairs={{0,7},{1,0},{2,1},{3,2},{4,3},{5,4},{6,5},{7,6},{8,15},{9,8},{10,9... | collective-permute-start | bytes 393224 | tf_op jit(solution)/shard_map/ppermute | solution.py:21
  28.9 6.5 %collective-permute-start.6 = (bf16[1,32,2048]{2,1,0:T(8,128)(2,1)S(1)}, bf16[1,32,2048]{2,1,0:T(8,128)(2,1)S(1)}, u32[]{:S(2)}, u32[]{:S(2)}) collective-permute-start(bf16[1,32,2048]{2,1,0:T(8,128)(2,1)S(1)} %collective-permute-done.4), channel_id=1, source_target_pairs={{0,1},{1,2},{2,3},{3,4},{4,5},{5,6},{6,7},{7,0},{8,9},{9,10},{10,1... | collective-permute-start | bytes 393224 | tf_op jit(solution)/shard_map/ppermute | solution.py:18
  49.4 5.7 %collective-permute-start.7 = (f32[1,256,10]{2,1,0:T(8,128)S(1)}, f32[1,256,10]{2,1,0:T(8,128)S(1)}, u32[]{:S(2)}, u32[]{:S(2)}) collective-permute-start(f32[1,256,10]{2,1,0:T(8,128)S(1)} %get-tuple-element.5), channel_id=1, source_target_pairs={{0,1},{1,2},{2,3},{3,4},{4,5},{5,6},{6,7},{8,9},{9,10},{10,11},{11... | collective-permute-start | bytes 30728 | tf_op jit(solution)/shard_map/ppermute | solution.py:35
  52.5 18.2 %copy-start.1 = (s32[8]{0:T(128)S(1)}, s32[8]{0:T(128)}, u32[]{:S(2)}) copy-start(s32[8]{0:T(128)} %param.5) | copy-start | bytes 100
  52.5 6.4 %collective-permute-start.8 = (f32[1,256,10]{2,1,0:T(8,128)S(1)}, f32[1,256,10]{2,1,0:T(8,128)S(1)}, u32[]{:S(2)}, u32[]{:S(2)}) collective-permute-start(f32[1,256,10]{2,1,0:T(8,128)S(1)} %get-tuple-element.6), channel_id=1, source_target_pairs={{1,0},{2,1},{3,2},{4,3},{5,4},{6,5},{7,6},{9,8},{10,9},{11,10},{12... | collective-permute-start | bytes 30728 | tf_op jit(solution)/shard_map/ppermute | solution.py:36
  66.7 106.6 %collective-permute-start.9 = (f32[1,256,285]{2,1,0:T(8,128)S(1)}, f32[1,256,285]{2,1,0:T(8,128)S(1)}, u32[]{:S(2)}, u32[]{:S(2)}) collective-permute-start(f32[1,256,285]{2,1,0:T(8,128)S(1)} %slice.186), channel_id=1, source_target_pairs={{0,1},{1,2},{2,3},{3,4},{4,5},{5,6},{6,7},{8,9},{9,10},{10,11},{11... | collective-permute-start | bytes 875528 | tf_op jit(solution)/shard_map/ppermute | solution.py:44
  173.4 5.7 %collective-permute-start.10 = (f32[1,19,1309]{2,1,0:T(8,128)S(1)}, f32[1,19,1309]{2,1,0:T(8,128)S(1)}, u32[]{:S(2)}, u32[]{:S(2)}) collective-permute-start(f32[1,19,1309]{2,1,0:T(8,128)S(1)} %fusion.345), channel_id=1, source_target_pairs={{0,8},{8,16},{16,24},{1,9},{9,17},{17,25},{2,10},{10,18},{18,26},{... | collective-permute-start | bytes 298460 | tf_op jit(solution)/shard_map/ppermute | solution.py:44
Sparse Core Ops, SparseCore 0:
  8.9 36.9 all-gather.1
